TPU v7x, 32 devices: a whole 2x2x4 slice. The times are simulated.
32 devices in a mesh: cuts: 4 (over z), blk: 2 (over x), rep: 4 (over y, core).
Axes of the slice: x: 2, y: 2, z: 4, core: 2. Of those that a mesh axis runs over, the one named last changes fastest.
Arguments:
- features: bfloat16 [8192, 256], P(('cuts', 'blk', 'rep')), may hold values from -6 to 6
- adj_values: bfloat16 [64, 4, 128, 1024], P(('cuts', 'blk'), 'rep'), as said below
- adj_cols: int32 [64, 4, 8], P(('cuts', 'blk'), 'rep'), may hold values from 0 to 15, as said below
- adj_count: int32 [64, 4], P(('cuts', 'blk'), 'rep'), may hold values from 1 to 8, as said below
- weight: bfloat16 [256, 256], replicated, may hold values from -0.375 to 0.375
- cotangent: bfloat16 [8192, 256], P(('cuts', 'blk', 'rep')), may hold values from -6 to 6
Outputs:
- output: bfloat16 [8192, 256], P(('cuts', 'blk', 'rep'))
- weight_grad: float32 [256, 256], replicated
Inputs may be any that keep to these rules, and one draw needn't show every extreme that they name: `adj_values`: entries are nonnegative; a row of a block has about 8 nonzero entries on average. `adj_cols`: within one row block and rep index the 8 numbers are distinct. `adj_count`: in every aligned group of 8 row blocks, for every rep index, some row block has count 8.
All inputs are finite; a program needn't handle non-finite values.
Results may differ from a plain program's by a relative error of at most 0.0061.
Values may be sent and summed in bfloat16 or wider, within the bound.
A program may use at most 64 MiB of HBM per device.

v0:
```python
import jax
import jax.numpy as jnp
from jax import lax
from jax.sharding import PartitionSpec as P


def silu_grad(pre):
    sigmoid_z = jax.nn.sigmoid(pre)
    return sigmoid_z * (1.0 + pre * (1.0 - sigmoid_z))


def local(features, adj_values, adj_cols, adj_count, weight, cotangent):
    block_size = adj_values.shape[2]
    slot_count = adj_cols.shape[2]
    feature_width = features.shape[1]
    group_rows = adj_values.shape[0]
    in_slice = lax.all_gather(features, "blk", axis=0, tiled=True)
    gathered = lax.all_gather(in_slice, "cuts", axis=0, tiled=True)
    panel_blocks = gathered.reshape(-1, block_size, feature_width)
    columns = adj_cols[:, 0, :]
    picked = panel_blocks[columns]
    slot_ids = jnp.arange(slot_count, dtype=jnp.int32)[None, :]
    usable = slot_ids < adj_count[:, 0][:, None]
    picked = jnp.where(usable[:, :, None, None], picked, jnp.zeros((), jnp.bfloat16))
    picked = picked.reshape(group_rows, slot_count * block_size, feature_width)
    partial_value = lax.dot_general(
        adj_values[:, 0], picked, (((2,), (1,)), ((0,), (0,))), preferred_element_type=jnp.float32
    )
    partial_value = partial_value.reshape(group_rows * block_size, feature_width)
    summed = lax.psum_scatter(partial_value, "rep", scatter_dimension=0, tiled=True)
    hidden = summed.astype(jnp.bfloat16)
    pre = jnp.dot(hidden, weight, preferred_element_type=jnp.float32)
    output = jax.nn.silu(pre).astype(jnp.bfloat16)
    grad_pre = (cotangent.astype(jnp.float32) * silu_grad(pre)).astype(jnp.bfloat16)
    local_grad = lax.dot_general(
        hidden, grad_pre, (((0,), (0,)), ((), ())), preferred_element_type=jnp.float32
    )
    weight_grad = lax.psum(local_grad, ("cuts", "blk", "rep"))
    return (output, weight_grad)


def solution(mesh):
    placed = (
        P(("cuts", "blk", "rep"), None),
        P(("cuts", "blk"), "rep", None, None),
        P(("cuts", "blk"), "rep", None),
        P(("cuts", "blk"), "rep"),
        P(),
        P(("cuts", "blk", "rep"), None),
    )
    return jax.shard_map(
        local,
        mesh=mesh,
        in_specs=placed,
        out_specs=(P(("cuts", "blk", "rep"), None), P()),
        check_vma=False,
    )
```

profile of v0, /device:TPU:0, one launch (start us, length us, event | category | flops | bytes accessed | tf_op | source)
XLA Modules:
  0.0 220.4 jit_solution(18052649329132863206)
XLA Ops:
  7.2 0.0 copy-start
  7.2 0.0 all-gather.2.cloned.1.call-start
  7.2 9.1 %all_gather.6 = bf16[512,256]{1,0:T(8,128)(2,1)} all-gather(bf16[256,256]{1,0:T(8,128)(2,1)} %param.6), channel_id=1, replica_groups=mesh['cuts'=4,'blk'=2,'rep'=4] {'blk'}, dimensions={0}, use_global_device_ids=true | all-gather | bytes 393216 | tf_op jit(solution)/shard_map/all_gather | solution.py:17
  16.4 0.0 all-gather.2.cloned.1.call-update
  16.4 0.0 reduce-scatter.2.cloned.1.call-start
  16.4 0.7 compare_select_fusion
  17.1 0.1 reshape.67
  17.2 0.7 iota_compare_fusion
  17.9 0.1 broadcast_bitcast_fusion
  18.0 26.9 %all-gather.2.cloned.1.call-done = bf16[2048,256]{1,0:T(8,128)(2,1)} async-done(((bf16[512,256]{1,0:T(8,128)(2,1)}), bf16[2048,256]{1,0:T(8,128)(2,1)}) %all-gather.2.cloned.1.call-update) | async-done | bytes 1048592 | tf_op jit(solution)/shard_map/all_gather | solution.py:18
  44.8 4.0 %gather_fusion = bf16[64,128,256]{2,1,0:T(8,128)(2,1)} fusion(bf16[16,128,256]{2,1,0:T(8,128)(2,1)} %bitcast.19, s32[1024]{0:T(1024)S(1)} %pad_clamp_fusion), kind=kCustom, calls=%fused_computation | custom fusion | bytes 8388864 | tf_op jit(solution)/shard_map/gather | solution.py:21
  48.8 4.6 %bitcast_select_fusion = bf16[8,1024,256]{2,1,0:T(8,128)(2,1)S(1)} fusion(pred[8,1024]{1,0:T(8,128)(4,1)S(1)} %broadcast_bitcast_fusion, bf16[8,1024,256]{2,1,0:T(8,128)(2,1)} %bitcast.18), kind=kLoop, calls=%fused_computation.1 | loop fusion | flops 2097152 | bytes 8396800 | tf_op jit(solution)/shard_map/jit(_where)/select_n | solution.py:24
  53.4 0.0 copy-done
  53.4 0.0 copy-start.1
  53.4 0.0 copy-start.2
  53.4 1.8 fusion
  55.2 0.0 reduce-scatter.2.cloned.1.call-update
  55.2 0.0 all-reduce.2.cloned.1.call-start
  55.3 24.2 %reduce-scatter.2.cloned.1.call-done = f32[256,256]{1,0:T(8,128)} async-done(((f32[1024,256]{1,0:T(8,128)}), f32[256,256]{1,0:T(8,128)}) %reduce-scatter.2.cloned.1.call-update) | async-done | bytes 262160 | tf_op jit(solution)/shard_map/reduce_scatter | solution.py:30
  79.5 0.0 copy-done.1
  79.5 1.8 multiply_convert_fusion.1
  81.4 0.0 copy-done.2
  81.4 1.9 fusion.2
  83.3 0.0 all-reduce.2.cloned.1.call-update
  83.3 128.8 %all-reduce.2.cloned.1.call-done = f32[256,256]{1,0:T(8,128)} async-done(((f32[256,256]{1,0:T(8,128)}), f32[256,256]{1,0:T(8,128)}) %all-reduce.2.cloned.1.call-update) | async-done | bytes 262160 | tf_op jit(solution)/shard_map/psum | solution.py:38
  212.2 1.7 copy.9
  (1 shorter events, 0.0 us)
Async XLA Ops:
  7.2 46.2 %copy-start = (bf16[8,1,128,1024]{3,2,1,0:T(8,128)(2,1)S(1)}, bf16[8,1,128,1024]{3,2,1,0:T(8,128)(2,1)}, u32[]{:S(2)}) copy-start(bf16[8,1,128,1024]{3,2,1,0:T(8,128)(2,1)} %param.7) | copy-start | bytes 6291460
  7.2 37.7 %all-gather.2.cloned.1.call-start = ((), (), s32[]{:S(2)}) async-start(), calls=%async_computation.1 | async-start | bytes 1310720 | tf_op jit(solution)/shard_map/all_gather | solution.py:18
  16.4 63.1 %reduce-scatter.2.cloned.1.call-start = ((), (), s32[]{:S(2)}) async-start(), calls=%async_computation.2 | async-start | bytes 1310720 | tf_op jit(solution)/shard_map/reduce_scatter | solution.py:30
  53.4 26.1 %copy-start.1 = (bf16[256,256]{1,0:T(8,128)(2,1)S(1)}, bf16[256,256]{1,0:T(8,128)(2,1)}, u32[]{:S(2)}) copy-start(bf16[256,256]{1,0:T(8,128)(2,1)} %param.10) | copy-start | bytes 393220
  53.4 27.9 %copy-start.2 = (bf16[256,256]{1,0:T(8,128)(2,1)S(1)}, bf16[256,256]{1,0:T(8,128)(2,1)}, u32[]{:S(2)}) copy-start(bf16[256,256]{1,0:T(8,128)(2,1)} %param.11) | copy-start | bytes 393220
  55.2 157.0 %all-reduce.2.cloned.1.call-start = ((), (), s32[]{:S(2)}) async-start(), calls=%async_computation.3 | async-start | bytes 524288 | tf_op jit(solution)/shard_map/psum | solution.py:38
Sparse Core Ops, SparseCore 0:
  16.5 28.2 all-gather.1
  55.3 24.1 reduce-scatter.1
  85.6 126.5 all-reduce.1
where the time goes:
time: 221 us; the launch traced here: 220 us
  waiting for transfers between devices  180 us (81%)
  between operations  13.8 us (6%)
  blocking collectives  9.13 us (4%)
  other arithmetic  5.95 us (3%)
  local copies, waits for them, and re-layouts  5.83 us (3%)
  matrix products  5.53 us (3%)
    psum x1, waiting for transfers between devices, local(): weight_grad = lax.psum(local_grad, ('cuts', 'blk', 'rep'))  129 us
    all_gather x1, waiting for transfers between devices, local(): gathered = lax.all_gather(in_slice, 'cuts', axis=0, tiled=True)  26.9 us
    reduce_scatter x1, waiting for transfers between devices, local(): lax.psum_scatter(partial_value, 'rep', scatter_dimension=0, tiled=True)  24.2 us
    all_gather x1, blocking collectives, local(): in_slice = lax.all_gather(features, 'blk', axis=0, tiled=True)  9.13 us
    select_n x1, other arithmetic, local(): jnp.where(usable[:, :, None, None], picked, jnp.zeros((), jnp.bfloat16))  4.58 us
  transfers between devices with their start and end apart: 3, of which 3 were waited for; matrix products, arithmetic and copies ran while one was open for 1% of the time, Pallas kernels for 0%

commit v1 on v0

--- a/solution.py
+++ b/solution.py
@@ -1,7 +1,15 @@
+import functools
+
 import jax
 import jax.numpy as jnp
 from jax import lax
+from jax.experimental import pallas as pl
+from jax.experimental.pallas import tpu as pltpu
 from jax.sharding import PartitionSpec as P
+
+MESH = pl.DeviceIdType.MESH
+BF = jnp.bfloat16
+F32 = jnp.float32
 
 
 def silu_grad(pre):
@@ -39,6 +47,305 @@
     return (output, weight_grad)
 
 
+def fused_kernel(
+    nz, rows, slots, bs,
+    feat_ref, adj_ref, cols_ref, count_ref, w_ref, cot_ref,
+    out_ref, wg_ref,
+    panel, adjv, dense, acc, wv, cotv, b1s, b1r, b2s, b2r, hid, stage, parts, gath,
+    local_sem, adj_sem, a_send, a_recv, b_send, b_recv, d_send, d_recv,
+):
+    z = lax.axis_index("cuts")
+    x = lax.axis_index("blk")
+    r = lax.axis_index("rep")
+    nx, nrep = 2, 4
+    ndev = nz * nx * nrep
+    me = (z * nx + x) * nrep + r
+    own = z * nx + x
+
+    def coords(p):
+        return (p // (nx * nrep), (p // nrep) % nx, p % nrep)
+
+    barrier = pltpu.get_barrier_semaphore()
+
+    def greet(k, carry):
+        pl.semaphore_signal(
+            barrier, inc=1, device_id=coords((me + k) % ndev), device_id_type=MESH
+        )
+        return carry
+
+    lax.fori_loop(1, ndev, greet, 0)
+    own_copy = pltpu.make_async_copy(feat_ref, panel.at[own], local_sem.at[0])
+    own_copy.start()
+    adj_copies = [
+        pltpu.make_async_copy(
+            adj_ref.at[:, 0, :, pl.ds(k * bs, bs)], adjv.at[k], adj_sem.at[k]
+        )
+        for k in range(slots)
+    ]
+    for copy in adj_copies:
+        copy.start()
+    w_copy = pltpu.make_async_copy(w_ref, wv, local_sem.at[1])
+    w_copy.start()
+    cot_copy = pltpu.make_async_copy(cot_ref, cotv, local_sem.at[2])
+    cot_copy.start()
+    own_copy.wait()
+    pl.semaphore_wait(barrier, ndev - 1)
+
+    def hop(direction, src_z, src_x, c):
+        target = ((z + 1, x, r), (z - 1, x, r), (z, 1 - x, r))[direction]
+        piece = panel.at[src_z * nx + src_x, pl.ds(c * bs, bs)]
+        return pltpu.make_async_remote_copy(
+            src_ref=piece,
+            dst_ref=piece,
+            send_sem=a_send.at[direction, src_z, c],
+            recv_sem=a_recv.at[src_z * nx + src_x, c],
+            device_id=target,
+            device_id_type=MESH,
+        )
+
+    def arrive(src_z, src_x, c):
+        hop(2, src_z, src_x, c).wait_recv()
+
+    for c in range(2):
+        @pl.when(z < nz - 1)
+        def _():
+            hop(0, z, x, c).start()
+
+        @pl.when(z > 0)
+        def _():
+            hop(1, z, x, c).start()
+
+        hop(2, z, x, c).start()
+
+    for copy in adj_copies:
+        copy.wait()
+
+    def spread(t, carry):
+        i = t // nz // nx
+        s = t % (nz * nx)
+        count = count_ref[i]
+        for c in range(2):
+            q = s * 2 + c
+            slot = jnp.int32(0)
+            used = jnp.int32(0)
+            for k in range(slots):
+                hit = jnp.where((cols_ref[i, 0, k] == q) & (k < count), 1, 0)
+                slot = slot + hit * k
+                used = used + hit
+            block = adjv[slot, i]
+            scale = used.astype(F32).astype(BF)
+            dense[s, pl.ds(pl.multiple_of(i * bs, bs), bs), c * bs:(c + 1) * bs] = block * scale
+        return carry
+
+    lax.fori_loop(0, rows * nz * nx, spread, 0)
+
+    def multiply(s, first=False):
+        def tile(t, carry):
+            a = dense[s, pl.ds(pl.multiple_of(t * 2 * bs, 2 * bs), 2 * bs), :]
+            product = jnp.dot(a, panel[s], preferred_element_type=F32)
+            if first:
+                acc[t] = product
+            else:
+                acc[t] = acc[t] + product
+            return carry
+
+        lax.fori_loop(0, nrep, tile, 0)
+
+    multiply(own, first=True)
+    for d in range(1, nz + 1):
+        for c in range(2):
+            @pl.when(z - d >= 0)
+            def _():
+                arrive(z - d, x, c)
+
+                @pl.when(z < nz - 1)
+                def _():
+                    hop(0, z - d, x, c).start()
+
+                hop(2, z - d, x, c).start()
+
+            @pl.when(z + d < nz)
+            def _():
+                arrive(z + d, x, c)
+
+                @pl.when(z > 0)
+                def _():
+                    hop(1, z + d, x, c).start()
+
+                hop(2, z + d, x, c).start()
+
+        @pl.when(z - d >= 0)
+        def _():
+            multiply((z - d) * nx + x)
+
+        @pl.when(z + d < nz)
+        def _():
+            multiply((z + d) * nx + x)
+
+        for src_z in ((z,) if d == 1 else (z - d + 1, z + d - 1)):
+            @pl.when((src_z >= 0) & (src_z < nz))
+            def _():
+                for c in range(2):
+                    arrive(src_z, 1 - x, c)
+                multiply(src_z * nx + 1 - x)
+
+    y = r // 2
+    core = r % 2
+    mate = y * 2 + 1 - core
+    cross = (1 - y) * 2 + core
+    far = (1 - y) * 2 + 1 - core
+
+    def to_mate(k):
+        return pltpu.make_async_remote_copy(
+            src_ref=b1s.at[k], dst_ref=b1r.at[k],
+            send_sem=b_send.at[k], recv_sem=b_recv.at[k],
+            device_id=(z, x, mate), device_id_type=MESH,
+        )
+
+    def to_cross(c):
+        piece = pl.ds(c * bs, bs)
+        return pltpu.make_async_remote_copy(
+            src_ref=b2s.at[piece], dst_ref=b2r.at[piece],
+            send_sem=b_send.at[2 + c], recv_sem=b_recv.at[2 + c],
+            device_id=(z, x, cross), device_id_type=MESH,
+        )
+
+    b1s[0] = acc[far].astype(BF)
+    to_mate(0).start()
+    b1s[1] = acc[mate].astype(BF)
+    to_mate(1).start()
+    to_mate(0).wait_recv()
+    for c in range(2):
+        piece = slice(c * bs, (c + 1) * bs)
+        b2s[piece] = (acc[cross, piece] + b1r[0, piece].astype(F32)).astype(BF)
+        to_cross(c).start()
+    to_mate(1).wait_recv()
+    w_copy.wait()
+    cot_copy.wait()
+    for c in range(2):
+        piece = slice(c * bs, (c + 1) * bs)
+        known = acc[r, piece] + b1r[1, piece].astype(F32)
+        to_cross(c).wait_recv()
+        hid[piece] = (known + b2r[piece].astype(F32)).astype(BF)
+    hidden = hid[...]
+    pre = jnp.dot(hidden, wv[...], preferred_element_type=F32)
+    sigmoid_z = 1.0 / (1.0 + jnp.exp(-pre))
+    grad_pre = (
+        cotv[...].astype(F32) * (sigmoid_z * (1.0 + pre * (1.0 - sigmoid_z)))
+    ).astype(BF)
+    grad = lax.dot_general(
+        hidden, grad_pre, (((0,), (0,)), ((), ())), preferred_element_type=F32
+    ).astype(BF)
+    tall = 16
+    for p in range(ndev):
+        stage[p] = grad[p // 2 * tall:(p // 2 + 1) * tall, p % 2 * 128:(p % 2 + 1) * 128]
+
+    def scatter(k):
+        p = (me + k) % ndev
+        return pltpu.make_async_remote_copy(
+            src_ref=stage.at[p], dst_ref=parts.at[k],
+            send_sem=d_send.at[0], recv_sem=d_recv.at[0],
+            device_id=coords(p), device_id_type=MESH,
+        )
+
+    def spray(k):
+        p = (me + k) % ndev
+        return pltpu.make_async_remote_copy(
+            src_ref=gath.at[me], dst_ref=gath.at[me],
+            send_sem=d_send.at[1], recv_sem=d_recv.at[1],
+            device_id=coords(p), device_id_type=MESH,
+        )
+
+    def everyone(send):
+        def one(k, carry):
+            send(k).start()
+            return carry
+
+        lax.fori_loop(1, ndev, one, 0)
+
+    def all_of(buf, k):
+        whole = buf.at[pl.ds(1, ndev - 1)]
+        return pltpu.make_async_remote_copy(
+            src_ref=whole, dst_ref=whole,
+            send_sem=d_send.at[k], recv_sem=d_recv.at[k],
+            device_id=(z, x, mate), device_id_type=MESH,
+        )
+
+    everyone(scatter)
+    out_ref[...] = (pre * sigmoid_z).astype(BF)
+    total = stage[me].astype(F32)
+    all_of(parts, 0).wait_recv()
+    for k in range(1, ndev):
+        total = total + parts[k].astype(F32)
+    gath[me] = total.astype(BF)
+    everyone(spray)
+
+    for k in range(2):
+        to_mate(k).wait_send()
+        to_cross(k).wait_send()
+    for c in range(2):
+        for src in range(nz):
+            @pl.when((z < nz - 1) & (src <= z))
+            def _():
+                hop(0, src, x, c).wait_send()
+
+            @pl.when((z > 0) & (src >= z))
+            def _():
+                hop(1, src, x, c).wait_send()
+
+            hop(2, src, x, c).wait_send()
+    all_of(stage, 0).wait_send()
+    all_of(gath, 1).wait_recv()
+    for p in range(ndev):
+        wg_ref[p // 2 * tall:(p // 2 + 1) * tall, p % 2 * 128:(p % 2 + 1) * 128] = gath[p].astype(F32)
+    all_of(gath, 1).wait_send()
+
+
+def fused(nz, features, adj_values, adj_cols, adj_count, weight, cotangent):
+    rows, _, bs, wide = adj_values.shape
+    slots = wide // bs
+    width = features.shape[1]
+    ndev = nz * 8
+    hbm = pl.BlockSpec(memory_space=pl.ANY)
+    smem = pl.BlockSpec(memory_space=pltpu.SMEM)
+    vmem = pl.BlockSpec(memory_space=pltpu.VMEM)
+    own = features.shape[0]
+    return pl.pallas_call(
+        functools.partial(fused_kernel, nz, rows, slots, bs),
+        out_shape=(
+            jax.ShapeDtypeStruct(features.shape, BF),
+            jax.ShapeDtypeStruct(weight.shape, F32),
+        ),
+        in_specs=[hbm, hbm, smem, smem, hbm, hbm],
+        out_specs=(vmem, vmem),
+        scratch_shapes=[
+            pltpu.VMEM((nz * 2, own, width), BF),
+            pltpu.VMEM((slots, rows, bs, bs), BF),
+            pltpu.VMEM((nz * 2, rows * bs, own), BF),
+            pltpu.VMEM((4, own, width), F32),
+            pltpu.VMEM(weight.shape, BF),
+            pltpu.VMEM((own, width), BF),
+            pltpu.VMEM((2, own, width), BF),
+            pltpu.VMEM((2, own, width), BF),
+            pltpu.VMEM((own, width), BF),
+            pltpu.VMEM((own, width), BF),
+            pltpu.VMEM((own, width), BF),
+            pltpu.VMEM((ndev, 16, 128), BF),
+            pltpu.VMEM((ndev, 16, 128), BF),
+            pltpu.VMEM((ndev, 16, 128), BF),
+            pltpu.SemaphoreType.DMA((3,)),
+            pltpu.SemaphoreType.DMA((slots,)),
+            pltpu.SemaphoreType.DMA((3, nz, 2)),
+            pltpu.SemaphoreType.DMA((nz * 2, 2)),
+            pltpu.SemaphoreType.DMA((4,)),
+            pltpu.SemaphoreType.DMA((4,)),
+            pltpu.SemaphoreType.DMA((2,)),
+            pltpu.SemaphoreType.DMA((2,)),
+        ],
+        compiler_params=pltpu.CompilerParams(collective_id=0, has_side_effects=True),
+    )(features, adj_values, adj_cols, adj_count.reshape(-1), weight, cotangent)
+
+
 def solution(mesh):
     placed = (
         P(("cuts", "blk", "rep"), None),
@@ -48,8 +355,10 @@
         P(),
         P(("cuts", "blk", "rep"), None),
     )
+    sizes = (mesh.shape["cuts"], mesh.shape["blk"], mesh.shape["rep"])
+    body = functools.partial(fused, sizes[0]) if sizes == (4, 2, 4) else local
     return jax.shard_map(
-        local,
+        body,
         mesh=mesh,
         in_specs=placed,
         out_specs=(P(("cuts", "blk", "rep"), None), P()),

time: 221 us -> 45.7 us (0.21)
  waiting for transfers between devices: 180 us -> 0 us
  Pallas kernels: 0 us -> 41.6 us
  between operations: 13.8 us -> 0.64 us
  blocking collectives: 9.13 us -> 0 us
  other arithmetic: 5.95 us -> 0 us
  matrix products: 5.53 us -> 0 us
  local copies, waits for them, and re-layouts: 5.83 us -> 3.24 us
    psum x1 -> x0, waiting for transfers between devices: 129 us -> none  [local(): weight_grad = lax.psum(local_grad, ('cuts', 'blk', 'rep'))]
    pallas_call x0 -> x1, Pallas kernels: none -> 41.6 us  [fused(): pl.pallas_call(functools.partial(fused_kernel, nz, rows, slots, bs), out_...]
    all_gather x1 -> x0, waiting for transfers between devices: 26.9 us -> none  [local(): gathered = lax.all_gather(in_slice, 'cuts', axis=0, tiled=True)]
    reduce_scatter x1 -> x0, waiting for transfers between devices: 24.2 us -> none  [local(): lax.psum_scatter(partial_value, 'rep', scatter_dimension=0, tiled=True)]
    all_gather x1 -> x0, blocking collectives: 9.13 us -> none  [local(): in_slice = lax.all_gather(features, 'blk', axis=0, tiled=True)]
    dot_general x3 -> x0, matrix products: 5.53 us -> none  [the longest x1 1.93 us: local(): lax.dot_general(hidden, grad_pre, (((0,), (0,)), ((), ())), preferred_ele...]
    select_n x2 -> x0, other arithmetic: 5.27 us -> none  [the longest x1 4.58 us: local(): jnp.where(usable[:, :, None, None], picked, jnp.zeros((), jnp.bfloat16))]
    gather x1 -> x0, local copies, waits for them, and re-layouts: 3.98 us -> none  [local(): picked = panel_blocks[columns]]
  transfers between devices with their start and end apart: 3 -> 0, of which waited for: 3 -> 0; matrix products, arithmetic and copies ran while one was open for 1% -> 0% of each run, Pallas kernels for 0% -> 0%
where the time goes in v1:
time: 45.7 us; the launch traced here: 45.5 us
  Pallas kernels  41.6 us (91%)
  local copies, waits for them, and re-layouts  3.24 us (7%)
  between operations  0.64 us (1%)
    pallas_call x1, Pallas kernels, fused(): pl.pallas_call(functools.partial(fused_kernel, nz, rows, slots, bs), out_...  41.6 us
    unnamed x2, local copies, waits for them, and re-layouts  3.24 us

profile of v1, /device:TPU:0, one launch (start us, length us, event | category | flops | bytes accessed | tf_op | source)
XLA Modules:
  0.0 45.5 jit_solution(2122709396565987707)
XLA Ops:
  0.6 41.6 %shard_map.77 = (bf16[256,256]{1,0:T(8,128)(2,1)}, f32[256,256]{1,0:T(8,128)}) custom-call(bf16[256,256]{1,0:T(8,128)(2,1)} %feat_ref.1, bf16[8,1,128,1024]{3,2,1,0:T(8,128)(2,1)} %adj_ref.1, s32[8,1,8]{2,1,0:T(1,128)} %cols_ref.1, s32[8]{0:T(128)} %bitcast.1, bf16[256,256]{1,0:T(8,128)(2,1)} %w_ref.1, bf16[256,256]{1,0:T(8,128)(2,1)} %cot_ref.1), custom_call_target="tpu_custom_call" | custom-call | tf_op jit(solution)/shard_map/pallas_call | solution.py:313
  42.3 1.6 %copy.10 = bf16[256,256]{1,0:T(8,128)(2,1)} copy(bf16[256,256]{1,0:T(8,128)(2,1)} %get-tuple-element.4) | data formatting | bytes 262144
  43.8 1.7 %copy.11 = f32[256,256]{1,0:T(8,128)} copy(f32[256,256]{1,0:T(8,128)} %get-tuple-element.5) | data formatting | bytes 524288

commit v2 on v1

--- a/solution.py
+++ b/solution.py
@@ -50,8 +50,8 @@
 def fused_kernel(
     nz, rows, slots, bs,
     feat_ref, adj_ref, cols_ref, count_ref, w_ref, cot_ref,
-    out_ref, wg_ref,
-    panel, adjv, dense, acc, wv, cotv, b1s, b1r, b2s, b2r, hid, stage, parts, gath,
+    out_ref, sum_ref,
+    panel, adjv, dense, acc, wv, cotv, b1s, b1r, b2s, b2r, hid, outv, stage, parts, gath,
     local_sem, adj_sem, a_send, a_recv, b_send, b_recv, d_send, d_recv,
 ):
     z = lax.axis_index("cuts")
@@ -65,15 +65,28 @@
     def coords(p):
         return (p // (nx * nrep), (p // nrep) % nx, p % nrep)
 
+    y = r // 2
+    core = r % 2
+    mate = y * 2 + 1 - core
+    cross = (1 - y) * 2 + core
+    far = (1 - y) * 2 + 1 - core
+
     barrier = pltpu.get_barrier_semaphore()
 
-    def greet(k, carry):
-        pl.semaphore_signal(
-            barrier, inc=1, device_id=coords((me + k) % ndev), device_id_type=MESH
-        )
-        return carry
-
-    lax.fori_loop(1, ndev, greet, 0)
+    def greet(device):
+        pl.semaphore_signal(barrier, inc=1, device_id=device, device_id_type=MESH)
+
+    @pl.when(z < nz - 1)
+    def _():
+        greet((z + 1, x, r))
+
+    @pl.when(z > 0)
+    def _():
+        greet((z - 1, x, r))
+
+    greet((z, 1 - x, r))
+    greet((z, x, mate))
+    greet((z, x, cross))
     own_copy = pltpu.make_async_copy(feat_ref, panel.at[own], local_sem.at[0])
     own_copy.start()
     adj_copies = [
@@ -89,15 +102,24 @@
     cot_copy = pltpu.make_async_copy(cot_ref, cotv, local_sem.at[2])
     cot_copy.start()
     own_copy.wait()
-    pl.semaphore_wait(barrier, ndev - 1)
+    @pl.when((z > 0) & (z < nz - 1))
+    def _():
+        pl.semaphore_wait(barrier, 5)
+
+    @pl.when((z == 0) | (z == nz - 1))
+    def _():
+        pl.semaphore_wait(barrier, 4)
+
+    pieces = 4
+    step = 2 * bs // pieces
 
     def hop(direction, src_z, src_x, c):
         target = ((z + 1, x, r), (z - 1, x, r), (z, 1 - x, r))[direction]
-        piece = panel.at[src_z * nx + src_x, pl.ds(c * bs, bs)]
+        piece = panel.at[src_z * nx + src_x, pl.ds(c * step, step)]
         return pltpu.make_async_remote_copy(
             src_ref=piece,
             dst_ref=piece,
-            send_sem=a_send.at[direction, src_z, c],
+            send_sem=a_send.at[direction, src_z * nx + src_x, c],
             recv_sem=a_recv.at[src_z * nx + src_x, c],
             device_id=target,
             device_id_type=MESH,
@@ -106,7 +128,7 @@
     def arrive(src_z, src_x, c):
         hop(2, src_z, src_x, c).wait_recv()
 
-    for c in range(2):
+    for c, across in zip(range(pieces), (2, 3, 0, 1)):
         @pl.when(z < nz - 1)
         def _():
             hop(0, z, x, c).start()
@@ -115,30 +137,37 @@
         def _():
             hop(1, z, x, c).start()
 
-        hop(2, z, x, c).start()
+        hop(2, z, x, across).start()
 
     for copy in adj_copies:
         copy.wait()
 
-    def spread(t, carry):
-        i = t // nz // nx
-        s = t % (nz * nx)
-        count = count_ref[i]
-        for c in range(2):
-            q = s * 2 + c
-            slot = jnp.int32(0)
-            used = jnp.int32(0)
-            for k in range(slots):
-                hit = jnp.where((cols_ref[i, 0, k] == q) & (k < count), 1, 0)
-                slot = slot + hit * k
-                used = used + hit
-            block = adjv[slot, i]
-            scale = used.astype(F32).astype(BF)
-            dense[s, pl.ds(pl.multiple_of(i * bs, bs), bs), c * bs:(c + 1) * bs] = block * scale
-        return carry
-
-    lax.fori_loop(0, rows * nz * nx, spread, 0)
-
+    def spread(src_z, src_x):
+        s = src_z * nx + src_x
+
+        def one(i, carry):
+            count = count_ref[i]
+            for c in range(2):
+                q = s * 2 + c
+                slot = jnp.int32(0)
+                used = jnp.int32(0)
+                for k in range(slots):
+                    hit = jnp.where((cols_ref[i, 0, k] == q) & (k < count), 1, 0)
+                    slot = slot + hit * k
+                    used = used + hit
+                block = adjv[slot, i]
+                scale = used.astype(F32).astype(BF)
+                dense[s, pl.ds(pl.multiple_of(i * bs, bs), bs), c * bs:(c + 1) * bs] = block * scale
+            return carry
+
+        lax.fori_loop(0, rows, one, 0, unroll=2)
+
+    order = (
+        (z, x), (z, 1 - x),
+        ((z + 1) % nz, x), ((z + nz - 1) % nz, x),
+        ((z + 1) % nz, 1 - x), ((z + nz - 1) % nz, 1 - x),
+        ((z + 2) % nz, x), ((z + 2) % nz, 1 - x),
+    )
     def multiply(s, first=False):
         def tile(t, carry):
             a = dense[s, pl.ds(pl.multiple_of(t * 2 * bs, 2 * bs), 2 * bs), :]
@@ -151,9 +180,12 @@
 
         lax.fori_loop(0, nrep, tile, 0)
 
-    multiply(own, first=True)
-    for d in range(1, nz + 1):
-        for c in range(2):
+    spread(*order[0])
+    spread(*order[1])
+    for d in range(1, nz):
+        for c in range(pieces):
+            late = False
+
             @pl.when(z - d >= 0)
             def _():
                 arrive(z - d, x, c)
@@ -162,7 +194,12 @@
                 def _():
                     hop(0, z - d, x, c).start()
 
-                hop(2, z - d, x, c).start()
+                if late:
+                    @pl.when(z - d > 0)
+                    def _():
+                        hop(2, z - d, x, c).start()
+                else:
+                    hop(2, z - d, x, c).start()
 
             @pl.when(z + d < nz)
             def _():
@@ -172,7 +209,31 @@
                 def _():
                     hop(1, z + d, x, c).start()
 
-                hop(2, z + d, x, c).start()
+                if late:
+                    @pl.when(z + d < nz - 1)
+                    def _():
+                        hop(2, z + d, x, c).start()
+                else:
+                    hop(2, z + d, x, c).start()
+
+            if False:
+                @pl.when(z + d - 1 == nz - 1)
+                def _():
+                    arrive(nz - 1, 1 - x, c + pieces // 2)
+                    hop(1, nz - 1, 1 - x, c + pieces // 2).start()
+
+                @pl.when(z - (d - 1) == 0)
+                def _():
+                    arrive(0, 1 - x, c + pieces // 2)
+                    hop(0, 0, 1 - x, c + pieces // 2).start()
+
+            if d == 1:
+                if c < 2:
+                    spread(*order[2 + c])
+                elif c == 2:
+                    multiply(own, first=True)
+            elif d == 2:
+                spread(*order[4 + c])
 
         @pl.when(z - d >= 0)
         def _():
@@ -182,18 +243,27 @@
         def _():
             multiply((z + d) * nx + x)
 
-        for src_z in ((z,) if d == 1 else (z - d + 1, z + d - 1)):
+        near = d - 1
+        for src_z in ((z,) if d == 1 else (z - near, z + near)):
             @pl.when((src_z >= 0) & (src_z < nz))
             def _():
-                for c in range(2):
-                    arrive(src_z, 1 - x, c)
+                for c in range(pieces):
+                    if False:
+                        passed = (src_z == nz - 1) | (src_z == 0)
+
+                        @pl.when(jnp.logical_not(passed))
+                        def _():
+                            arrive(src_z, 1 - x, c)
+                    else:
+                        arrive(src_z, 1 - x, c)
                 multiply(src_z * nx + 1 - x)
 
-    y = r // 2
-    core = r % 2
-    mate = y * 2 + 1 - core
-    cross = (1 - y) * 2 + core
-    far = (1 - y) * 2 + 1 - core
+    for src_z in (z - (nz - 1), z + nz - 1):
+        @pl.when((src_z >= 0) & (src_z < nz))
+        def _():
+            for c in range(pieces):
+                arrive(src_z, 1 - x, c)
+            multiply(src_z * nx + 1 - x)
 
     def to_mate(k):
         return pltpu.make_async_remote_copy(
@@ -236,54 +306,113 @@
     grad = lax.dot_general(
         hidden, grad_pre, (((0,), (0,)), ((), ())), preferred_element_type=F32
     ).astype(BF)
+    stage[...] = grad
+
     tall = 16
-    for p in range(ndev):
-        stage[p] = grad[p // 2 * tall:(p // 2 + 1) * tall, p % 2 * 128:(p % 2 + 1) * 128]
-
-    def scatter(k):
-        p = (me + k) % ndev
+    owners = nx * nrep
+    place = x * nrep + r
+    owns = (z == 1) | (z == 2)
+    quad = owners // 2
+
+    def rank(owner_z, p):
+        return p % 2 * owners + (owner_z - 1) * quad + p // 2
+
+    def rows_of(o, n=1):
+        return pl.ds(pl.multiple_of(o * tall, tall), n * tall)
+
+    mine = rows_of(rank(jnp.clip(z, 1, 2), place))
+    half = rows_of(core * owners, owners)
+
+    def scatter(target_z, p):
+        o = target_z * owners + p
         return pltpu.make_async_remote_copy(
-            src_ref=stage.at[p], dst_ref=parts.at[k],
+            src_ref=stage.at[rows_of(rank(target_z, p))],
+            dst_ref=parts.at[(o - me + ndev) % ndev],
             send_sem=d_send.at[0], recv_sem=d_recv.at[0],
-            device_id=coords(p), device_id_type=MESH,
-        )
-
-    def spray(k):
-        p = (me + k) % ndev
+            device_id=(target_z, p // nrep, p % nrep), device_id_type=MESH,
+        )
+
+    def spray(target_z, q):
         return pltpu.make_async_remote_copy(
-            src_ref=gath.at[me], dst_ref=gath.at[me],
+            src_ref=gath.at[mine], dst_ref=gath.at[mine],
             send_sem=d_send.at[1], recv_sem=d_recv.at[1],
-            device_id=coords(p), device_id_type=MESH,
-        )
-
-    def everyone(send):
+            device_id=(target_z, q // 2, q % 2 * 2 + core), device_id_type=MESH,
+        )
+
+    def chips(target_z, whole):
+        for k in range(0 if whole else 1, quad):
+            spray(target_z, (place // 2 + k) % quad).start()
+
+    hand_over = pltpu.make_async_remote_copy(
+        src_ref=gath.at[half], dst_ref=gath.at[half],
+        send_sem=d_send.at[2], recv_sem=d_recv.at[2],
+        device_id=(z, x, mate), device_id_type=MESH,
+    )
+
+    def plane(send, target_z, whole):
         def one(k, carry):
-            send(k).start()
+            send(target_z, (place + k) % owners).start()
             return carry
 
-        lax.fori_loop(1, ndev, one, 0)
-
-    def all_of(buf, k):
-        whole = buf.at[pl.ds(1, ndev - 1)]
+        lax.fori_loop(0 if whole else 1, owners, one, 0, unroll=True)
+
+    def many(whole, k):
         return pltpu.make_async_remote_copy(
             src_ref=whole, dst_ref=whole,
             send_sem=d_send.at[k], recv_sem=d_recv.at[k],
             device_id=(z, x, mate), device_id_type=MESH,
         )
 
-    everyone(scatter)
-    out_ref[...] = (pre * sigmoid_z).astype(BF)
-    total = stage[me].astype(F32)
-    all_of(parts, 0).wait_recv()
-    for k in range(1, ndev):
-        total = total + parts[k].astype(F32)
-    gath[me] = total.astype(BF)
-    everyone(spray)
-
+    @pl.when(z < 2)
+    def _():
+        plane(scatter, 2, True)
+
+    @pl.when(z >= 2)
+    def _():
+        plane(scatter, 1, True)
+
+    @pl.when(z == 0)
+    def _():
+        plane(scatter, 1, True)
+
+    @pl.when(z == nz - 1)
+    def _():
+        plane(scatter, 2, True)
+
+    @pl.when(owns)
+    def _():
+        plane(scatter, z, False)
+
+    outv[...] = (pre * sigmoid_z).astype(BF)
+    out_copy = pltpu.make_async_copy(outv, out_ref, local_sem.at[3])
+    out_copy.start()
+
+    all_parts = parts.at[pl.ds(1, ndev - 1)]
+    all_but_one = stage.at[pl.ds(0, (2 * owners - 1) * tall)]
+
+    @pl.when(owns)
+    def _():
+        total = stage[mine, :].astype(F32)
+        many(all_parts, 0).wait_recv()
+        for k in range(1, ndev):
+            total = total + parts[k].astype(F32)
+        gath[mine, :] = total.astype(BF)
+        chips(3 * (2 - z), True)
+        chips(3 - z, True)
+        chips(3 * (z - 1), True)
+        chips(z, False)
+        many(gath.at[pl.ds(0, (owners - 1) * tall)], 1).wait_recv()
+
+    @pl.when(jnp.logical_not(owns))
+    def _():
+        many(gath.at[pl.ds(0, owners * tall)], 1).wait_recv()
+
+    hand_over.start()
     for k in range(2):
         to_mate(k).wait_send()
         to_cross(k).wait_send()
-    for c in range(2):
+    for c in range(pieces):
+        late = False
         for src in range(nz):
             @pl.when((z < nz - 1) & (src <= z))
             def _():
@@ -293,12 +422,50 @@
             def _():
                 hop(1, src, x, c).wait_send()
 
-            hop(2, src, x, c).wait_send()
-    all_of(stage, 0).wait_send()
-    all_of(gath, 1).wait_recv()
-    for p in range(ndev):
-        wg_ref[p // 2 * tall:(p // 2 + 1) * tall, p % 2 * 128:(p % 2 + 1) * 128] = gath[p].astype(F32)
-    all_of(gath, 1).wait_send()
+            if late and src in (0, nz - 1):
+                @pl.when(z == src)
+                def _():
+                    hop(2, src, x, c).wait_send()
+            else:
+                hop(2, src, x, c).wait_send()
+        if late:
+            @pl.when(z < nz - 1)
+            def _():
+                hop(0, 0, 1 - x, c).wait_send()
+
+            @pl.when(z > 0)
+            def _():
+                hop(1, nz - 1, 1 - x, c).wait_send()
+
+    @pl.when(owns)
+    def _():
+        many(all_but_one, 0).wait_send()
+        many(all_but_one, 1).wait_send()
+
+    @pl.when(jnp.logical_not(owns))
+    def _():
+        many(stage, 0).wait_send()
+
+    hand_over.wait_send()
+    hand_over.wait_recv()
+    sum_ref[...] = gath[...]
+    out_copy.wait()
+
+
+def finish_kernel(out_in, sum_in, out_ref, wg_ref, outv, sumv, wgv, sems):
+    sum_get = pltpu.make_async_copy(sum_in, sumv, sems.at[0])
+    out_get = pltpu.make_async_copy(out_in, outv, sems.at[1])
+    sum_get.start()
+    out_get.start()
+    sum_get.wait()
+    wgv[...] = sumv[...].astype(F32)
+    wg_put = pltpu.make_async_copy(wgv, wg_ref, sems.at[2])
+    wg_put.start()
+    out_get.wait()
+    out_put = pltpu.make_async_copy(outv, out_ref, sems.at[3])
+    out_put.start()
+    wg_put.wait()
+    out_put.wait()
 
 
 def fused(nz, features, adj_values, adj_cols, adj_count, weight, cotangent):
@@ -310,14 +477,14 @@
     smem = pl.BlockSpec(memory_space=pltpu.SMEM)
     vmem = pl.BlockSpec(memory_space=pltpu.VMEM)
     own = features.shape[0]
-    return pl.pallas_call(
+    out, total = pl.pallas_call(
         functools.partial(fused_kernel, nz, rows, slots, bs),
         out_shape=(
             jax.ShapeDtypeStruct(features.shape, BF),
-            jax.ShapeDtypeStruct(weight.shape, F32),
+            jax.ShapeDtypeStruct(weight.shape, BF),
         ),
         in_specs=[hbm, hbm, smem, smem, hbm, hbm],
-        out_specs=(vmem, vmem),
+        out_specs=(hbm, vmem),
         scratch_shapes=[
             pltpu.VMEM((nz * 2, own, width), BF),
             pltpu.VMEM((slots, rows, bs, bs), BF),
@@ -330,20 +497,36 @@
             pltpu.VMEM((own, width), BF),
             pltpu.VMEM((own, width), BF),
             pltpu.VMEM((own, width), BF),
-            pltpu.VMEM((ndev, 16, 128), BF),
-            pltpu.VMEM((ndev, 16, 128), BF),
-            pltpu.VMEM((ndev, 16, 128), BF),
-            pltpu.SemaphoreType.DMA((3,)),
+            pltpu.VMEM((own, width), BF),
+            pltpu.VMEM(weight.shape, BF),
+            pltpu.VMEM((ndev, 16, width), BF),
+            pltpu.VMEM(weight.shape, BF),
+            pltpu.SemaphoreType.DMA((4,)),
             pltpu.SemaphoreType.DMA((slots,)),
-            pltpu.SemaphoreType.DMA((3, nz, 2)),
-            pltpu.SemaphoreType.DMA((nz * 2, 2)),
+            pltpu.SemaphoreType.DMA((3, nz * 2, 4)),
+            pltpu.SemaphoreType.DMA((nz * 2, 4)),
             pltpu.SemaphoreType.DMA((4,)),
             pltpu.SemaphoreType.DMA((4,)),
-            pltpu.SemaphoreType.DMA((2,)),
-            pltpu.SemaphoreType.DMA((2,)),
+            pltpu.SemaphoreType.DMA((3,)),
+            pltpu.SemaphoreType.DMA((3,)),
         ],
         compiler_params=pltpu.CompilerParams(collective_id=0, has_side_effects=True),
     )(features, adj_values, adj_cols, adj_count.reshape(-1), weight, cotangent)
+    return pl.pallas_call(
+        finish_kernel,
+        out_shape=(
+            jax.ShapeDtypeStruct(out.shape, BF),
+            jax.ShapeDtypeStruct(total.shape, F32),
+        ),
+        in_specs=[hbm, hbm],
+        out_specs=(hbm, hbm),
+        scratch_shapes=[
+            pltpu.VMEM(out.shape, BF),
+            pltpu.VMEM(total.shape, BF),
+            pltpu.VMEM(total.shape, F32),
+            pltpu.SemaphoreType.DMA((4,)),
+        ],
+    )(out, total)
 
 
 def solution(mesh):

time: 45.7 us -> 42.6 us (0.932)
  local copies, waits for them, and re-layouts: 3.24 us -> 0 us
    unnamed x2 -> x0, local copies, waits for them, and re-layouts: 3.24 us -> none
    pallas_call x0 -> x1, Pallas kernels: none -> 1.7 us  [fused(): pl.pallas_call(finish_kernel, out_shape=(jax.ShapeDtypeStruct(out.shape,...]
    pallas_call x1, Pallas kernels: 41.6 us -> 40.1 us  [fused(): pl.pallas_call(functools.partial(fused_kernel, nz, rows, slots, bs), out_...]
where the time goes in v2:
time: 42.6 us; the launch traced here: 42.4 us
  Pallas kernels  41.8 us (98%)
  between operations  0.64 us (2%)
    pallas_call x1, Pallas kernels, fused(): pl.pallas_call(functools.partial(fused_kernel, nz, rows, slots, bs), out_...  40.1 us
    pallas_call x1, Pallas kernels, fused(): pl.pallas_call(finish_kernel, out_shape=(jax.ShapeDtypeStruct(out.shape,...  1.7 us

profile of v2, /device:TPU:0, one launch (start us, length us, event | category | flops | bytes accessed | tf_op | source)
XLA Modules:
  0.0 42.4 jit_solution(6071284665173863085)
XLA Ops:
  0.6 40.1 %shard_map.77 = (bf16[256,256]{1,0:T(8,128)(2,1)}, bf16[256,256]{1,0:T(8,128)(2,1)}) custom-call(bf16[256,256]{1,0:T(8,128)(2,1)} %feat_ref.1, bf16[8,1,128,1024]{3,2,1,0:T(8,128)(2,1)} %adj_ref.1, s32[8,1,8]{2,1,0:T(1,128)} %cols_ref.1, s32[8]{0:T(128)} %bitcast.1, bf16[256,256]{1,0:T(8,128)(2,1)} %w_ref.1, bf16[256,256]{1,0:T(8,128)(2,1)} %cot_ref.1), custom_call_target="tpu_custom_call" | custom-call | tf_op jit(solution)/shard_map/pallas_call | solution.py:480
  40.7 1.7 %shard_map.78 = (bf16[256,256]{1,0:T(8,128)(2,1)}, f32[256,256]{1,0:T(8,128)}) custom-call(bf16[256,256]{1,0:T(8,128)(2,1)} %get-tuple-element.4.out_in, bf16[256,256]{1,0:T(8,128)(2,1)} %get-tuple-element.5.sum_in), custom_call_target="tpu_custom_call" | custom-call | tf_op jit(solution)/shard_map/pallas_call | solution.py:515
